TPU v7x, 512 devices: a whole 4x8x8 slice. The times are simulated.
512 devices in a mesh: row: 32 (over z_lo, x, core), col: 16 (over z_hi, y).
Axes of the slice: x: 4, y: 8, z: 8 (z_hi: 2, z_lo: 4; z = z_hi * 4 + z_lo), core: 2. Of those that a mesh axis runs over, the one named last changes fastest.
Arguments:
- state: float32 [32, 2, 16, 256, 256], P('row', None, 'col'), may hold values from -6 to 6
- a_tiles: float32 [32, 2, 16, 256, 256], P('row', None, 'col'), may hold values from -0.375 to 0.375
- inverses: float32 [32, 256, 256], P('row'), may hold values from -0.225 to 1.025
Outputs:
- state_out: float32 [32, 2, 16, 256, 256], P('row', None, 'col')
All inputs are finite; a program needn't handle non-finite values.
Results may differ from a plain program's by a relative error of at most 0.0001.
Values sent between devices are 32-bit elements; how exact they have to be, the bound alone decides.
A program may use at most 64 MiB of HBM per device.

v0:
```python
import jax
import jax.numpy as jnp
from jax import lax
from jax.sharding import PartitionSpec as P

FRONTS = 3
DOUBLINGS = 5


HIGH = lax.Precision.HIGHEST
shift_half = 0.5


def swapped(value, axis, stride):
    mask = 2**stride
    pairs = [(source, source ^ mask) for source in range(lax.axis_size(axis))]
    return lax.ppermute(value, axis, pairs)


def passed_along(block, axis, distance):
    devices = range(lax.axis_size(axis))
    route = [((i - distance) % len(devices), i) for i in devices]
    return lax.ppermute(block, axis, route)


def spread(value, axis, source):
    kept = jnp.where(lax.axis_index(axis) == source, value, 0).astype(value.dtype)
    return lax.psum(kept, axis)


def product(left, right):
    return jnp.dot(left, right, precision=HIGH, preferred_element_type=jnp.float32)


def product_transposed(left, right):
    return lax.dot_general(
        left, right, (((1,), (1,)), ((), ())), precision=HIGH, preferred_element_type=jnp.float32
    )


def batched_product(left, right):
    return jnp.einsum(
        "nab,nbc->nac", left, right, precision=HIGH, preferred_element_type=jnp.float32
    )


def across_cols(pieces):
    return lax.all_to_all(pieces, "col", split_axis=1, concat_axis=1, tiled=True)


def mirrored(tile_set):
    slot_count = tile_set.shape[0]
    tile_order = tile_set.shape[1]
    col_count = lax.axis_size("col")
    slab_rows = tile_order // col_count
    section_one = across_cols(tile_set.reshape(slot_count, col_count, slab_rows, tile_order))
    by_target = section_one.reshape(slot_count * col_count, slab_rows, tile_order)
    section_two = lax.all_to_all(by_target, "row", split_axis=0, concat_axis=0, tiled=True)
    section_three = across_cols(section_two.reshape(slot_count, col_count, slab_rows, tile_order))
    return section_three.reshape(slot_count, tile_order, tile_order)


def flipped(tile_set, col_count):
    levels = col_count.bit_length() - 1
    for bit_pos in range(levels):
        tile_set = swapped(tile_set, "col", bit_pos)
    return tile_set


def per_device(state, a_tiles, inverses):
    slot_count = state.shape[1]
    tile_order = state.shape[3]
    col_count = lax.axis_size("col")
    height = lax.axis_size("row")
    row_here = lax.axis_index("row")
    col_here = lax.axis_index("col")
    current = state.reshape(slot_count, tile_order, tile_order)
    coupling = a_tiles.reshape(slot_count, tile_order, tile_order)
    own_inverse = inverses.reshape(tile_order, tile_order)
    identity_tile = jnp.eye(tile_order, dtype=jnp.float32)
    left_powers = [identity_tile - shift_half * own_inverse]
    for level in range(DOUBLINGS - 1):
        left_powers.append(product(left_powers[-1], left_powers[-1]))
    column_inverse = mirrored(jnp.broadcast_to(own_inverse, (slot_count, tile_order, tile_order)))
    right_list = [identity_tile[None] - shift_half * column_inverse]
    for level in range(DOUBLINGS - 1):
        right_list.append(batched_product(right_list[-1], right_list[-1]))
    right_powers = jnp.stack(right_list)
    tile_cols = jnp.arange(slot_count, dtype=jnp.int32) * col_count + col_here
    tile_sum = row_here + tile_cols
    for front_step in range(FRONTS):
        front_sum = height - 1 - front_step
        source_a = flipped(coupling, col_count)
        if front_step > 0:
            source_a = passed_along(source_a, "col", -front_step)
        front_col = front_sum - row_here
        front_slot = jnp.clip(front_col // col_count, 0, slot_count - 1)
        own_tile = lax.dynamic_index_in_dim(current, front_slot, 0, keepdims=False)
        mirror = mirrored(current)
        far_tile = lax.dynamic_index_in_dim(mirror, front_slot, 0, keepdims=False)
        right_side = own_tile + far_tile.T
        right_inverse = lax.dynamic_index_in_dim(column_inverse, front_slot, 0, keepdims=False)
        powers_here = lax.dynamic_index_in_dim(right_powers, front_slot, 1, keepdims=False)
        solution = shift_half * product_transposed(product(own_inverse, right_side), right_inverse)
        for level in range(DOUBLINGS):
            solution = solution + product_transposed(
                product(left_powers[level], solution), powers_here[level]
            )
        passed = []
        for slot_pos in range(slot_count):
            root_row = jnp.clip(front_sum - tile_cols[slot_pos], 0, height - 1)
            passed.append(spread(solution, "row", root_row))
        below_rows = front_sum - tile_cols
        a_slot = jnp.clip(below_rows // col_count, 0, slot_count - 1)
        a_pick = jnp.take(source_a, a_slot, axis=0)
        update = batched_product(a_pick, jnp.stack(passed))
        shrink = (tile_sum < front_sum)[:, None, None]
        place = (tile_sum == front_sum)[:, None, None]
        current = jnp.where(shrink, current - update, jnp.where(place, solution[None], current))
    return current.reshape(state.shape)


def solution(mesh):
    in_specs = (
        P("row", None, "col", None, None),
        P("row", None, "col", None, None),
        P("row", None, None),
    )
    out_specs = P("row", None, "col", None, None)
    return jax.shard_map(
        per_device, mesh=mesh, in_specs=in_specs, out_specs=out_specs, check_vma=False
    )
```

profile of v0, /device:TPU:1, one launch (start us, length us, event | category | flops | bytes accessed | tf_op | source)
XLA Modules:
  0.0 1221.0 jit_solution(3985047102242037960)
XLA Ops:
  6.5 1.1 copy.25
  7.6 34.1 %all_to_all.60 = f32[2,16,16,256]{3,2,0,1:T(8,128)S(1)} all-to-all(f32[2,16,16,256]{3,2,0,1:T(8,128)S(1)} %copy.25), channel_id=1, replica_groups=mesh['row'=32,'col'=16] {'col'}, dimensions={1} | all-to-all | bytes 1048576 | tf_op jit(solution)/shard_map/all_to_all | solution.py:48
  41.7 1.8 broadcast_in_dim.91
  43.5 5.7 all-to-all-start.3
  49.2 0.8 copy.26
  50.0 16.1 %all-to-all-done.3 = f32[2,16,16,256]{3,2,0,1:T(8,128)S(1)} async-done(((f32[2,16,16,256]{3,2,0,1:T(8,128)}), f32[2,16,16,256]{3,2,0,1:T(8,128)S(1)}, u32[]{:S(2)}, u32[]{:S(2)}) %all-to-all-start.3) | async-done | bytes 524320 | tf_op jit(solution)/shard_map/all_to_all | solution.py:48
  66.1 10.6 all-to-all-start.1
  76.8 0.8 copy.30
  77.6 15.6 %all-to-all-done.1 = f32[32,16,256]{2,1,0:T(8,128)S(1)} async-done(((f32[32,16,256]{2,1,0:T(8,128)}), f32[32,16,256]{2,1,0:T(8,128)S(1)}, u32[]{:S(2)}, u32[]{:S(2)}) %all-to-all-start.1) | async-done | bytes 524320 | tf_op jit(solution)/shard_map/all_to_all | solution.py:58
  93.2 4.1 all-to-all-start.4
  97.3 3.2 collective-permute-start
  100.5 0.8 copy.27
  101.4 12.4 %all-to-all-done.4 = f32[32,16,256]{2,1,0:T(8,128)S(1)} async-done(((f32[32,16,256]{2,1,0:T(8,128)}), f32[32,16,256]{2,1,0:T(8,128)S(1)}, u32[]{:S(2)}, u32[]{:S(2)}) %all-to-all-start.4) | async-done | bytes 524320 | tf_op jit(solution)/shard_map/all_to_all | solution.py:58
  113.7 4.5 all-to-all-start.2
  118.7 4.2 collective-permute-start.1
  123.3 0.8 copy.31
  124.1 13.2 %all-to-all-done.2 = f32[2,16,16,256]{3,2,0,1:T(8,128)S(1)} async-done(((f32[2,16,16,256]{3,2,0,1:T(8,128)}), f32[2,16,16,256]{3,2,0,1:T(8,128)S(1)}, u32[]{:S(2)}, u32[]{:S(2)}) %all-to-all-start.2) | async-done | bytes 524320 | tf_op jit(solution)/shard_map/all_to_all | solution.py:48
  137.4 5.7 all-to-all-start.5
  143.1 0.6 fusion.92
  143.8 15.3 %collective-permute-done.1 = f32[2,256,256]{2,1,0:T(8,128)} collective-permute-done((f32[2,256,256]{2,1,0:T(8,128)}, f32[2,256,256]{2,1,0:T(8,128)}, u32[]{:S(2)}, u32[]{:S(2)}) %collective-permute-start.1) | collective-permute-done | bytes 524320 | tf_op jit(solution)/shard_map/ppermute | solution.py:17
  159.0 8.0 collective-permute-start.2
  169.1 20.2 %collective-permute-done.2 = f32[2,256,256]{2,1,0:T(8,128)} collective-permute-done((f32[2,256,256]{2,1,0:T(8,128)}, f32[2,256,256]{2,1,0:T(8,128)}, u32[]{:S(2)}, u32[]{:S(2)}) %collective-permute-start.2) | collective-permute-done | bytes 524320 | tf_op jit(solution)/shard_map/ppermute | solution.py:17
  189.3 2.1 collective-permute-start.3
  191.6 0.6 fusion.20
  192.2 0.6 convolution_multiply_fusion.2
  193.4 0.7 bitcast_dynamic-update-slice_fusion.2
  194.1 0.7 bitcast_dynamic-update-slice_fusion.1
  194.8 0.7 bitcast_dynamic-update-slice_fusion
  195.5 0.7 fusion.4
  197.8 0.4 convolution_add_fusion.12
  199.4 0.4 convolution_add_fusion.10
  199.8 0.8 select_bitcast_fusion.5
  200.8 11.9 collective-permute-done.3
  212.7 2.4 gather_fusion
  215.1 269.7 %all-reduce.11.cloned.1.call-done = (f32[1,256,256]{2,1,0:T(8,128)}, f32[1,256,256]{2,1,0:T(8,128)}) async-done(((f32[1,256,256]{2,1,0:T(8,128)}, f32[1,256,256]{2,1,0:T(8,128)}), (f32[1,256,256]{2,1,0:T(8,128)}, f32[1,256,256]{2,1,0:T(8,128)})) %all-reduce.11.cloned.1.call-update) | async-done | bytes 524304 | tf_op jit(solution)/shard_map/psum | solution.py:28
  484.8 1.9 fusion.3
  486.7 26.0 %all_to_all.61 = f32[2,16,16,256]{3,2,0,1:T(8,128)S(1)} all-to-all(f32[2,16,16,256]{3,2,0,1:T(8,128)S(1)} %copy.34), channel_id=1, replica_groups=mesh['row'=32,'col'=16] {'col'}, dimensions={1} | all-to-all | bytes 1048576 | tf_op jit(solution)/shard_map/all_to_all | solution.py:48
  512.8 23.9 %all_to_all.62 = f32[32,16,256]{2,1,0:T(8,128)S(1)} all-to-all(f32[32,16,256]{2,1,0:T(8,128)S(1)} %bitcast.223), channel_id=1, replica_groups=mesh['row'=32,'col'=16] {'row'}, dimensions={0} | all-to-all | bytes 1048576 | tf_op jit(solution)/shard_map/all_to_all | solution.py:58
  536.7 0.8 copy.36
  537.5 4.9 all-to-all-start.8
  543.8 9.5 collective-permute-start.4
  553.3 8.2 all-to-all-done.8
  561.7 0.6 fusion.25
  562.4 0.6 convolution_multiply_fusion.1
  565.1 0.4 convolution_add_fusion.7
  566.7 0.4 convolution_add_fusion.5
  567.2 0.8 select_bitcast_fusion.3
  568.1 9.1 collective-permute-done.4
  577.1 2.4 gather_fusion.1
  579.5 270.4 %all-reduce.9.cloned.1.call-done = (f32[1,256,256]{2,1,0:T(8,128)}, f32[1,256,256]{2,1,0:T(8,128)}) async-done(((f32[1,256,256]{2,1,0:T(8,128)}, f32[1,256,256]{2,1,0:T(8,128)}), (f32[1,256,256]{2,1,0:T(8,128)}, f32[1,256,256]{2,1,0:T(8,128)})) %all-reduce.9.cloned.1.call-update) | async-done | bytes 524304 | tf_op jit(solution)/shard_map/psum | solution.py:28
  850.0 1.9 fusion.2
  851.9 26.0 %all_to_all.63 = f32[2,16,16,256]{3,2,0,1:T(8,128)S(1)} all-to-all(f32[2,16,16,256]{3,2,0,1:T(8,128)S(1)} %copy.39), channel_id=1, replica_groups=mesh['row'=32,'col'=16] {'col'}, dimensions={1} | all-to-all | bytes 1048576 | tf_op jit(solution)/shard_map/all_to_all | solution.py:48
  878.0 23.9 %all_to_all.64 = f32[32,16,256]{2,1,0:T(8,128)S(1)} all-to-all(f32[32,16,256]{2,1,0:T(8,128)S(1)} %bitcast.225), channel_id=1, replica_groups=mesh['row'=32,'col'=16] {'row'}, dimensions={0} | all-to-all | bytes 1048576 | tf_op jit(solution)/shard_map/all_to_all | solution.py:58
  901.9 0.8 copy.41
  902.8 4.9 all-to-all-start.11
  909.0 10.5 collective-permute-start.5
  919.4 7.3 all-to-all-done.11
  927.0 0.6 fusion.22
  927.6 0.6 convolution_multiply_fusion
  932.4 0.8 select_bitcast_fusion.1
  933.3 11.4 collective-permute-done.5
  944.7 0.6 gather_fusion.2
  945.3 266.6 %all-reduce.7.cloned.1.call-done = (f32[1,256,256]{2,1,0:T(8,128)}, f32[1,256,256]{2,1,0:T(8,128)}) async-done(((f32[1,256,256]{2,1,0:T(8,128)}, f32[1,256,256]{2,1,0:T(8,128)}), (f32[1,256,256]{2,1,0:T(8,128)}, f32[1,256,256]{2,1,0:T(8,128)})) %all-reduce.7.cloned.1.call-update) | async-done | bytes 524304 | tf_op jit(solution)/shard_map/psum | solution.py:28
  1211.9 2.5 fusion.1
  (80 shorter events, 13.4 us)
Async XLA Ops:
  43.5 53.8 %copy-start.5 = (f32[1,2,1,256,256]{4,3,2,1,0:T(8,128)S(1)}, f32[1,2,1,256,256]{4,3,2,1,0:T(8,128)}, u32[]{:S(2)}) copy-start(f32[1,2,1,256,256]{4,3,2,1,0:T(8,128)} %param.6) | copy-start | bytes 1572868
  43.5 22.6 %all-to-all-start.3 = ((f32[2,16,16,256]{3,2,0,1:T(8,128)}), f32[2,16,16,256]{3,2,0,1:T(8,128)S(1)}, u32[]{:S(2)}, u32[]{:S(2)}) async-start(f32[2,16,16,256]{3,2,0,1:T(8,128)} %broadcast_in_dim.91), calls=%async_computation.3 | async-start | bytes 1048576 | tf_op jit(solution)/shard_map/all_to_all | solution.py:48
  66.1 52.2 %copy-start = (f32[1,256,256]{2,1,0:T(8,128)S(1)}, f32[1,256,256]{2,1,0:T(8,128)}, u32[]{:S(2)}) copy-start(f32[1,256,256]{2,1,0:T(8,128)} %param.7) | copy-start | bytes 786436
  66.1 27.1 %all-to-all-start.1 = ((f32[32,16,256]{2,1,0:T(8,128)}), f32[32,16,256]{2,1,0:T(8,128)S(1)}, u32[]{:S(2)}, u32[]{:S(2)}) async-start(f32[32,16,256]{2,1,0:T(8,128)} %bitcast.5), calls=%async_computation.1 | async-start | bytes 1048576 | tf_op jit(solution)/shard_map/all_to_all | solution.py:58
  93.2 20.6 %all-to-all-start.4 = ((f32[32,16,256]{2,1,0:T(8,128)}), f32[32,16,256]{2,1,0:T(8,128)S(1)}, u32[]{:S(2)}, u32[]{:S(2)}) async-start(f32[32,16,256]{2,1,0:T(8,128)} %bitcast.12), calls=%async_computation.4 | async-start | bytes 1048576 | tf_op jit(solution)/shard_map/all_to_all | solution.py:58
  97.3 21.4 %collective-permute-start = (f32[2,256,256]{2,1,0:T(8,128)S(1)}, f32[2,256,256]{2,1,0:T(8,128)}, u32[]{:S(2)}, u32[]{:S(2)}) collective-permute-start(f32[2,256,256]{2,1,0:T(8,128)S(1)} %bitcast.230), channel_id=1, source_target_pairs={{0,1},{1,0},{2,3},{3,2},{4,5},{5,4},{6,7},{7,6},{8,9},{9,8},{10,11... | collective-permute-start | bytes 1572872 | tf_op jit(solution)/shard_map/ppermute | solution.py:17
  113.7 23.6 %all-to-all-start.2 = ((f32[2,16,16,256]{3,2,0,1:T(8,128)}), f32[2,16,16,256]{3,2,0,1:T(8,128)S(1)}, u32[]{:S(2)}, u32[]{:S(2)}) async-start(f32[2,16,16,256]{3,2,0,1:T(8,128)} %copy.27), calls=%async_computation.2 | async-start | bytes 1048576 | tf_op jit(solution)/shard_map/all_to_all | solution.py:48
  118.7 40.3 %collective-permute-start.1 = (f32[2,256,256]{2,1,0:T(8,128)}, f32[2,256,256]{2,1,0:T(8,128)}, u32[]{:S(2)}, u32[]{:S(2)}) collective-permute-start(f32[2,256,256]{2,1,0:T(8,128)} %collective-permute-done), channel_id=1, source_target_pairs={{0,2},{1,3},{2,0},{3,1},{4,6},{5,7},{6,4},{7,5},{8,10},{9,11},{10,... | collective-permute-start | bytes 1572872 | tf_op jit(solution)/shard_map/ppermute | solution.py:17
  124.1 67.4 %copy-start.4 = (f32[1,2,1,256,256]{4,3,2,1,0:T(8,128)S(1)}, f32[1,2,1,256,256]{4,3,2,1,0:T(8,128)}, u32[]{:S(2)}) copy-start(f32[1,2,1,256,256]{4,3,2,1,0:T(8,128)} %param.5) | copy-start | bytes 1572868
  137.4 54.8 %all-to-all-start.5 = ((f32[2,16,16,256]{3,2,0,1:T(8,128)}), f32[2,16,16,256]{3,2,0,1:T(8,128)S(1)}, u32[]{:S(2)}, u32[]{:S(2)}) async-start(f32[2,16,16,256]{3,2,0,1:T(8,128)} %copy.31), calls=%async_computation.5 | async-start | bytes 1048576 | tf_op jit(solution)/shard_map/all_to_all | solution.py:48
  143.1 341.7 %all-reduce.11.cloned.1.call-start = ((), (), s32[]{:S(2)}) async-start(), calls=%async_computation.14 | async-start | bytes 1048576 | tf_op jit(solution)/shard_map/psum | solution.py:28
  159.0 30.2 %collective-permute-start.2 = (f32[2,256,256]{2,1,0:T(8,128)}, f32[2,256,256]{2,1,0:T(8,128)}, u32[]{:S(2)}, u32[]{:S(2)}) collective-permute-start(f32[2,256,256]{2,1,0:T(8,128)} %collective-permute-done.1), channel_id=1, source_target_pairs={{0,4},{1,5},{2,6},{3,7},{4,0},{5,1},{6,2},{7,3},{8,12},{9,13},{10,... | collective-permute-start | bytes 1572872 | tf_op jit(solution)/shard_map/ppermute | solution.py:17
  189.3 23.4 %collective-permute-start.3 = (f32[2,256,256]{2,1,0:T(8,128)}, f32[2,256,256]{2,1,0:T(8,128)}, u32[]{:S(2)}, u32[]{:S(2)}) collective-permute-start(f32[2,256,256]{2,1,0:T(8,128)} %collective-permute-done.2), channel_id=1, source_target_pairs={{0,8},{1,9},{2,10},{3,11},{4,12},{5,13},{6,14},{7,15},{8,0},{9,1},... | collective-permute-start | bytes 1572872 | tf_op jit(solution)/shard_map/ppermute | solution.py:17
  196.1 3.3 copy-start.1
  537.5 24.0 %all-to-all-start.8 = ((f32[2,16,16,256]{3,2,0,1:T(8,128)}), f32[2,16,16,256]{3,2,0,1:T(8,128)S(1)}, u32[]{:S(2)}, u32[]{:S(2)}) async-start(f32[2,16,16,256]{3,2,0,1:T(8,128)} %copy.36), calls=%async_computation.8 | async-start | bytes 1048576 | tf_op jit(solution)/shard_map/all_to_all | solution.py:48
  542.4 307.6 %all-reduce.9.cloned.1.call-start = ((), (), s32[]{:S(2)}) async-start(), calls=%async_computation.13 | async-start | bytes 1048576 | tf_op jit(solution)/shard_map/psum | solution.py:28
  543.8 33.4 %collective-permute-start.4 = (f32[2,256,256]{2,1,0:T(8,128)}, f32[2,256,256]{2,1,0:T(8,128)}, u32[]{:S(2)}, u32[]{:S(2)}) collective-permute-start(f32[2,256,256]{2,1,0:T(8,128)} %collective-permute-done.3), channel_id=1, source_target_pairs={{1,0},{2,1},{3,2},{4,3},{5,4},{6,5},{7,6},{8,7},{9,8},{10,9},{11,1... | collective-permute-start | bytes 1572872 | tf_op jit(solution)/shard_map/ppermute | solution.py:23
  561.7 1.7 copy-start.2
  902.8 24.0 %all-to-all-start.11 = ((f32[2,16,16,256]{3,2,0,1:T(8,128)}), f32[2,16,16,256]{3,2,0,1:T(8,128)S(1)}, u32[]{:S(2)}, u32[]{:S(2)}) async-start(f32[2,16,16,256]{3,2,0,1:T(8,128)} %copy.41), calls=%async_computation.11 | async-start | bytes 1048576 | tf_op jit(solution)/shard_map/all_to_all | solution.py:48
  907.6 304.3 %all-reduce.7.cloned.1.call-start = ((), (), s32[]{:S(2)}) async-start(), calls=%async_computation.12 | async-start | bytes 1048576 | tf_op jit(solution)/shard_map/psum | solution.py:28
  909.0 35.8 %collective-permute-start.5 = (f32[2,256,256]{2,1,0:T(8,128)}, f32[2,256,256]{2,1,0:T(8,128)S(1)}, u32[]{:S(2)}, u32[]{:S(2)}) collective-permute-start(f32[2,256,256]{2,1,0:T(8,128)} %collective-permute-done.3), channel_id=1, source_target_pairs={{2,0},{3,1},{4,2},{5,3},{6,4},{7,5},{8,6},{9,7},{10,8},{11,9},{12,... | collective-permute-start | bytes 1572872 | tf_op jit(solution)/shard_map/ppermute | solution.py:23
  926.9 1.7 copy-start.3
Sparse Core Ops, SparseCore 0:
  200.8 283.9 all-reduce.10
  568.1 281.8 all-reduce.8
  933.3 278.5 all-reduce.6
where the time goes:
time: 1220 us
  waiting for transfers between devices  948 us (78%)
  blocking collectives  134 us (11%)
  starting transfers between devices  77.9 us (6%)
  matrix products  26.2 us (2%)
  between operations  17.7 us (1%)
  local copies, waits for them, and re-layouts  14.9 us (1%)
    psum x3, waiting for transfers between devices, spread(): return lax.psum(kept, axis)  807 us
    all_to_all x3, blocking collectives, across_cols(): lax.all_to_all(pieces, 'col', split_axis=1, concat_axis=1, tiled=True)  86.2 us
    all_to_all x2, blocking collectives, mirrored(): lax.all_to_all(by_target, 'row', split_axis=0, concat_axis=0, tiled=True)  47.8 us
    ppermute x4, waiting for transfers between devices, swapped(): return lax.ppermute(value, axis, pairs)  47.4 us
    all_to_all x5, waiting for transfers between devices, across_cols(): lax.all_to_all(pieces, 'col', split_axis=1, concat_axis=1, tiled=True)  44.9 us
    all_to_all x2, waiting for transfers between devices, mirrored(): lax.all_to_all(by_target, 'row', split_axis=0, concat_axis=0, tiled=True)  28 us
    all_to_all x5, starting transfers between devices, across_cols(): lax.all_to_all(pieces, 'col', split_axis=1, concat_axis=1, tiled=True)  25.6 us
  transfers between devices with their start and end apart: 16, of which 14 were waited for; matrix products, arithmetic and copies ran while one was open for 3% of the time, Pallas kernels for 0%

commit v1 on v0

v1 whole, which is shorter than its diff:
```python
import functools

import jax
import jax.numpy as jnp
from jax import lax
from jax.experimental import pallas as pl
from jax.experimental.pallas import tpu as pltpu
from jax.sharding import PartitionSpec as P

FRONTS = 3
DOUBLINGS = 5
X_CHIPS = 4
F32 = jnp.float32
BF16 = jnp.bfloat16
MESH = pl.DeviceIdType.MESH


def split(value):
    high = value.astype(BF16)
    low = (value - high.astype(F32)).astype(BF16)
    return high, low


def dot(left, right):
    return jnp.dot(left, right, preferred_element_type=F32)


def product(left, right):
    return dot(left[0], right[0]) + (dot(left[0], right[1]) + dot(left[1], right[0]))


class Posted:
    def __init__(self, sems):
        self.sems = sems
        self.items = []

    def send(self, condition, src, dst, recv_sem, row, col):
        copy = pltpu.make_async_remote_copy(
            src_ref=src, dst_ref=dst, send_sem=self.sems.at[len(self.items)],
            recv_sem=recv_sem, device_id=(row, col), device_id_type=MESH,
        )
        self.items.append((condition, copy))

        @pl.when(condition)
        def _():
            copy.start()

    def drain(self):
        for condition, copy in self.items:
            @pl.when(condition)
            def _():
                copy.wait_send()


def landed(ref, sem):
    pltpu.make_async_copy(ref, ref, sem).wait()


N_SENDS = 192


def sweep(nt, nc, nx, state, coupling, inverse, out,
          flip, wide, inv_far, h_far, a_far, x_near, own, acc,
          left_hi, left_lo, right_hi, right_lo, tmp_hi, tmp_lo,
          send_sems, flip_sems, wide_sems, far_sems, near_sems):
    order = inverse.shape[-1]
    piece = order // nx
    per_plane = 2 * nx
    planes = nt // per_plane
    row, col = lax.axis_index("row"), lax.axis_index("col")
    plane, chip, core = row // per_plane, (row // 2) % nx, row % 2
    posted = Posted(send_sems)
    last = nt - 1
    lag = last - col - row
    role = [(lag == s) | (lag == s + nc) for s in range(FRONTS)]
    slot = jnp.where(lag >= nc, 1, 0)
    lags = [lag, lag - nc]

    def source_row(s, t):
        return last - s - nc * t - col

    for s in range(FRONTS):
        other = last - s - row
        posted.send(role[s] & (other != row), state.at[slot], h_far, far_sems.at[0], other, row % nc)
        posted.send((col == row % nc) & (other >= 0) & (other != row),
                    inverse, inv_far, far_sems.at[1], other, col)
        for step in range(1, s + 1):
            posted.send((col == (row + step) % nc) & (other >= 0) & (row + step <= last),
                        coupling.at[(row + step) // nc % 2], a_far.at[step - 1], far_sems.at[1 + step],
                        other, row % nc)

    for u in range(2):
        used = nc * u + col > row
        posted.send(used & (col != nc - 1) & (2 * col != nc - 2), coupling.at[u], flip.at[1, 1 - u],
                    flip_sems.at[1, 1 - u], row, nc - 2 - col)
    posted.send((col == nc - 1) & (last > row), coupling.at[1], flip.at[0, 0], flip_sems.at[0, 0], row, 0)
    for u in range(2):
        @pl.when((nc * u + col > row) & (2 * col == nc - 2))
        def _():
            flip[1, 1 - u] = coupling[u]

    @pl.when((nc - 1 > row) & (col == nc - 1))
    def _():
        flip[1, 0] = coupling[0]

    solver = role[0] | role[1] | role[2]
    flip_local = (2 * col == nc - 2) | (col == nc - 1)

    def hand_on(early):
        now = ~role[0] if early else role[0]
        for t in range(2):
            held = source_row(1, t) > row

            @pl.when(now & held & ~flip_local)
            def _():
                landed(flip.at[1, t], flip_sems.at[1, t])
            up = t + jnp.where(col == nc - 1, 1, 0)
            posted.send(now & held, flip.at[1, t], flip.at[0, up % 2], flip_sems.at[0, up % 2],
                        row, (col + 1) % nc)
            down = t - jnp.where(col == 0, 1, 0)
            posted.send(now & held & (down >= 0), flip.at[1, t], flip.at[2, down % 2],
                        flip_sems.at[2, down % 2], row, (col + nc - 1) % nc)

    hand_on(True)

    eye = (lax.broadcasted_iota(jnp.int32, (order, order), 0)
           == lax.broadcasted_iota(jnp.int32, (order, order), 1)).astype(F32)

    def powers(first, high, low):
        acc[...] = first

        def step(m, carry):
            value = split(acc[...])
            high[m], low[m] = value
            acc[...] = product(value, value)
            return carry
        lax.fori_loop(0, DOUBLINGS - 1, step, 0)
        high[DOUBLINGS - 1], low[DOUBLINGS - 1] = split(acc[...])

    self_mirror = role[1] & (2 * row == last - 1)
    mirrored = solver & ~self_mirror

    @pl.when(solver)
    def _():
        powers(eye - 0.5 * inverse[...], left_hi, left_lo)

        @pl.when(mirrored)
        def _():
            landed(inv_far, far_sems.at[1])

        @pl.when(self_mirror)
        def _():
            inv_far[...] = inverse[...]
            h_far[...] = state[slot]
        inv_far[...] = inv_far[...].T
        powers(eye - 0.5 * inv_far[...], right_hi, right_lo)

        @pl.when(mirrored)
        def _():
            landed(h_far, far_sems.at[0])
        acc[...] = state[slot] + h_far[...].T

    def transposed(ref):
        return split(ref[...].T)

    def solve():
        first = product(split(inverse[...]), split(acc[...]))
        own[...] = 0.5 * product(split(first), split(inv_far[...]))

        def level(m, carry):
            value = own[...]
            middle = product((left_hi[m], left_lo[m]), split(value))
            own[...] = value + product(split(middle), (right_hi[m], right_lo[m]))
            return carry
        lax.fori_loop(0, DOUBLINGS, level, 0)

    def spread(s):
        mirror = last - s - row
        for step in range(1, FRONTS - s):
            spot = 2 * (step - 1)
            if s + step == 2 and step == 1:
                spot = 0
            posted.send(role[s] & (row >= step), own, x_near.at[spot], near_sems.at[spot], row - step, col)
            posted.send(role[s] & (mirror >= step), own, x_near.at[spot + 1], near_sems.at[spot + 1],
                        row, (col + nc - step) % nc)
        for q in range(nx):
            posted.send(role[s] & (row >= 1) & (chip != q), own.at[pl.ds(q * piece, piece)],
                        wide.at[s, slot, pl.ds(q * piece, piece)], wide_sems.at[s, slot, q],
                        plane * per_plane + 2 * q + core, col)

    def relay(s):
        for t in range(2):
            src = source_row(s, t)
            top_plane, top_chip, side = src // per_plane, (src // 2) % nx, src % 2
            live = src >= 1
            here = live & (core == side)
            source = here & (row == src)
            level = here & (plane == top_plane)
            below = here & (plane < top_plane)
            span = pl.ds(pl.multiple_of(chip * piece, 8), piece)
            mine = wide.at[s, t, span]
            own_part = own.at[span]

            @pl.when((level & ~source) | below)
            def _():
                landed(mine, wide_sems.at[s, t, chip])
            for target in range(planes - 1):
                go = level & (target < top_plane)
                dst_row = target * per_plane + 2 * chip + core
                posted.send(go & ~source, mine, mine, wide_sems.at[s, t, chip], dst_row, col)
                posted.send(go & source, own_part, mine, wide_sems.at[s, t, chip], dst_row, col)
            for q in range(nx):
                go = (chip != q) & (below | (level & (q < top_chip)))
                dst_row = plane * per_plane + 2 * q + core
                posted.send(go & ~source, mine, mine, wide_sems.at[s, t, chip], dst_row, col)
                posted.send(go & source, own_part, mine, wide_sems.at[s, t, chip], dst_row, col)
            full = below | (level & (chip < top_chip))
            sibling = row + 1 - 2 * core
            for q in range(nx):
                part = wide.at[s, t, pl.ds(q * piece, piece)]

                @pl.when(full & (chip != q))
                def _():
                    landed(part, wide_sems.at[s, t, q])
                posted.send(full, part, part, wide_sems.at[s, t, q], sibling, col)
                posted.send(source & (side == 1), own.at[pl.ds(q * piece, piece)], part,
                            wide_sems.at[s, t, q], sibling, col)

    def leaf_wait(s, t):
        src = source_row(s, t)

        @pl.when((row < src) & (core != src % 2))
        def _():
            for q in range(nx):
                landed(wide.at[s, t, pl.ds(q * piece, piece)], wide_sems.at[s, t, q])

    def flip_wait(s, t):
        held = source_row(s, t) > row
        if s != 1:
            @pl.when(held)
            def _():
                landed(flip.at[s, t], flip_sems.at[s, t])

    @pl.when(role[0])
    def _():
        solve()
    spread(0)
    hand_on(False)
    relay(0)

    for t in range(2):
        for s in (0, 2):
            flip_wait(s, t)

    exists_row = row + 1 <= last
    @pl.when(role[1])
    def _():
        left = split(flip[0, slot])
        landed(a_far.at[0], far_sems.at[2])
        tmp_hi[...], tmp_lo[...] = transposed(a_far.at[0])
        landed(x_near.at[0], near_sems.at[0])
        acc[...] -= product(left, split(x_near[0]))
        landed(x_near.at[1], near_sems.at[1])
        acc[...] -= product(split(x_near[1]), (tmp_hi[...], tmp_lo[...]))
        solve()
    spread(1)
    relay(1)

    @pl.when(role[2])
    def _():
        landed(a_far.at[1], far_sems.at[3])
        tmp_hi[...], tmp_lo[...] = transposed(a_far.at[1])
        landed(x_near.at[2], near_sems.at[2])
        acc[...] -= product(split(flip[0, slot]), split(x_near[2]))
        landed(x_near.at[3], near_sems.at[3])
        acc[...] -= product(split(x_near[3]), (tmp_hi[...], tmp_lo[...]))
        landed(a_far.at[0], far_sems.at[2])
        tmp_hi[...], tmp_lo[...] = transposed(a_far.at[0])
        left = split(flip[1, slot])
        landed(x_near.at[0], near_sems.at[0])
        acc[...] -= product(left, split(x_near[0]))
        landed(x_near.at[1], near_sems.at[1])
        acc[...] -= product(split(x_near[1]), (tmp_hi[...], tmp_lo[...]))
        solve()
    spread(2)

    for s in range(FRONTS):
        if s == FRONTS - 1:
            relay(s)
        for t in range(2):
            leaf_wait(s, t)

            @pl.when(lags[t] >= FRONTS)
            def _():
                change = product(split(flip[s, t]), split(wide[s, t]))
                base = state[t] if s == 0 else out[t]
                out[t] = base - change
    for t in range(2):
        @pl.when(lags[t] < 0)
        def _():
            out[t] = state[t]

        @pl.when((lags[t] >= 0) & (lags[t] < FRONTS))
        def _():
            out[t] = own[...]
    posted.drain()


def per_device(nx, state, a_tiles, inverses):
    nc, nt = lax.axis_size("col"), lax.axis_size("row")
    order = inverses.shape[-1]
    tile = (order, order)
    in_vmem = pl.BlockSpec(memory_space=pltpu.VMEM)
    dma = pltpu.SemaphoreType.DMA
    result = pl.pallas_call(
        functools.partial(sweep, nt, nc, nx),
        out_shape=jax.ShapeDtypeStruct((2,) + tile, F32),
        in_specs=[in_vmem] * 3,
        out_specs=in_vmem,
        scratch_shapes=[
            pltpu.VMEM((FRONTS, 2) + tile, F32),
            pltpu.VMEM((FRONTS, 2) + tile, F32),
            pltpu.VMEM(tile, F32),
            pltpu.VMEM(tile, F32),
            pltpu.VMEM((2,) + tile, F32),
            pltpu.VMEM((4,) + tile, F32),
            pltpu.VMEM(tile, F32),
            pltpu.VMEM(tile, F32),
            pltpu.VMEM((DOUBLINGS,) + tile, BF16),
            pltpu.VMEM((DOUBLINGS,) + tile, BF16),
            pltpu.VMEM((DOUBLINGS,) + tile, BF16),
            pltpu.VMEM((DOUBLINGS,) + tile, BF16),
            pltpu.VMEM(tile, BF16),
            pltpu.VMEM(tile, BF16),
            dma((N_SENDS,)),
            dma((FRONTS, 2)),
            dma((FRONTS, 2, nx)),
            dma((4,)),
            dma((4,)),
        ],
        compiler_params=pltpu.CompilerParams(has_side_effects=True),
    )(state.reshape((2,) + tile), a_tiles.reshape((2,) + tile), inverses.reshape(tile))
    return result.reshape(state.shape)


def solution(mesh, nx=X_CHIPS):
    tiles = P("row", None, "col", None, None)
    return jax.shard_map(
        functools.partial(per_device, nx), mesh=mesh,
        in_specs=(tiles, tiles, P("row", None, None)), out_specs=tiles, check_vma=False,
    )
```

time: 1220 us -> 136 us (0.11)
  waiting for transfers between devices: 948 us -> 0 us
  Pallas kernels: 0 us -> 134 us
  blocking collectives: 134 us -> 0 us
  starting transfers between devices: 77.9 us -> 0 us
  matrix products: 26.2 us -> 0 us
  between operations: 17.7 us -> 0.01 us
  local copies, waits for them, and re-layouts: 14.9 us -> 1.87 us
    psum x3 -> x0, waiting for transfers between devices: 807 us -> none  [spread(): return lax.psum(kept, axis)]
    all_to_all x5 -> x0, blocking collectives: 134 us -> none  [the longest x3 86.2 us: across_cols(): lax.all_to_all(pieces, 'col', split_axis=1, concat_axis=1, tiled=True)]
    pallas_call x0 -> x1, Pallas kernels: none -> 134 us  [per_device(): pl.pallas_call(functools.partial(sweep, nt, nc, nx), out_shape=jax.ShapeD...]
    all_to_all x7 -> x0, waiting for transfers between devices: 72.9 us -> none  [the longest x5 44.9 us: across_cols(): lax.all_to_all(pieces, 'col', split_axis=1, concat_axis=1, tiled=True)]
    ppermute x6 -> x0, waiting for transfers between devices: 67.9 us -> none  [the longest x4 47.4 us: swapped(): return lax.ppermute(value, axis, pairs)]
    all_to_all x7 -> x0, starting transfers between devices: 40.4 us -> none  [the longest x5 25.6 us: across_cols(): lax.all_to_all(pieces, 'col', split_axis=1, concat_axis=1, tiled=True)]
    ppermute x6 -> x0, starting transfers between devices: 37.3 us -> none  [the longest x2 20 us: passed_along(): return lax.ppermute(block, axis, route)]
    dot_general x47 -> x0, matrix products: 26.2 us -> none  [the longest x22 9.1 us: product(): jnp.dot(left, right, precision=HIGH, preferred_element_type=jnp.float32)]
  transfers between devices with their start and end apart: 16 -> 0, of which waited for: 14 -> 0; matrix products, arithmetic and copies ran while one was open for 3% -> 0% of each run, Pallas kernels for 0% -> 0%
where the time goes in v1:
time: 136 us
  Pallas kernels  134 us (99%)
  local copies, waits for them, and re-layouts  1.87 us (1%)
    pallas_call x1, Pallas kernels, per_device(): pl.pallas_call(functools.partial(sweep, nt, nc, nx), out_shape=jax.ShapeD...  134 us

profile of v1, /device:TPU:1, one launch (start us, length us, event | category | flops | bytes accessed | tf_op | source)
XLA Modules:
  0.0 135.6 jit_solution(13915223201010649777)
XLA Ops:
  0.0 133.7 %shard_map.37 = f32[2,256,256]{2,1,0:T(8,128)} custom-call(f32[2,256,256]{2,1,0:T(8,128)} %bitcast.7, f32[2,256,256]{2,1,0:T(8,128)} %bitcast.8, f32[256,256]{1,0:T(8,128)} %bitcast.9), custom_call_target="tpu_custom_call" | custom-call | tf_op jit(solution)/shard_map/pallas_call | solution.py:315
  133.7 1.9 %copy.6 = f32[1,2,1,256,256]{4,3,2,1,0:T(8,128)} copy(f32[1,2,1,256,256]{4,3,2,1,0:T(8,128)} %bitcast.6) | data formatting | bytes 1048576

commit v2 on v1

--- a/solution.py
+++ b/solution.py
@@ -78,6 +78,51 @@
 
     def source_row(s, t):
         return last - s - nc * t - col
+
+    barrier = pltpu.get_barrier_semaphore()
+    greeted = []
+
+    def greet(condition, target_row, target_col):
+        @pl.when(condition)
+        def _():
+            pl.semaphore_signal(barrier, inc=1, device_id=(target_row, target_col), device_id_type=MESH)
+
+    def expect(condition):
+        greeted.append(jnp.where(condition, 1, 0))
+
+    for s in range(FRONTS):
+        other = last - s - row
+        apart = role[s] & (other != row)
+        greet(apart, other, row % nc)
+        expect(apart)
+        greet(apart, other, col)
+        expect((col == row % nc) & (other >= 0) & (other != row))
+        for step in range(1, s + 1):
+            greet(role[s], other, (other + step) % nc)
+            expect((col == (row + step) % nc) & (other >= 0) & (row + step <= last))
+            greet(role[s], row + step, col)
+            greet(role[s], row, (col + step) % nc)
+        for step in range(1, FRONTS - s):
+            expect(role[s] & (row >= step))
+            expect(role[s] & (other >= step))
+    paired = (col != nc - 1) & (2 * col != nc - 2)
+    greet(paired, row, nc - 2 - col)
+    expect(paired)
+    greet((col == 0) & (row < last), row, nc - 1)
+    expect((col == nc - 1) & (row < last))
+    every = row >= 0
+    for step in (1, nc - 1):
+        greet(every, row, (col + step) % nc)
+        expect(every)
+    for step in range(1, nx):
+        greet(every, plane * per_plane + (row + 2 * step) % per_plane, col)
+        expect(every)
+    for step in range(1, planes):
+        greet(every, (row + step * per_plane) % nt, col)
+        expect(every)
+    greet(every, row + 1 - 2 * core, col)
+    expect(every)
+    pl.semaphore_wait(barrier, functools.reduce(lambda x, y: x + y, greeted))
 
     for s in range(FRONTS):
         other = last - s - row
@@ -338,7 +383,7 @@
             dma((4,)),
             dma((4,)),
         ],
-        compiler_params=pltpu.CompilerParams(has_side_effects=True),
+        compiler_params=pltpu.CompilerParams(collective_id=0, has_side_effects=True),
     )(state.reshape((2,) + tile), a_tiles.reshape((2,) + tile), inverses.reshape(tile))
     return result.reshape(state.shape)
 

time: 136 us -> 127 us (0.934)
  Pallas kernels: 134 us -> 125 us
    pallas_call x1, Pallas kernels: 134 us -> 125 us  [per_device(): pl.pallas_call(functools.partial(sweep, nt, nc, nx), out_shape=jax.ShapeD...]
where the time goes in v2:
time: 127 us
  Pallas kernels  125 us (98%)
  local copies, waits for them, and re-layouts  1.87 us (1%)
    pallas_call x1, Pallas kernels, per_device(): pl.pallas_call(functools.partial(sweep, nt, nc, nx), out_shape=jax.ShapeD...  125 us

profile of v2, /device:TPU:1, one launch (start us, length us, event | category | flops | bytes accessed | tf_op | source)
XLA Modules:
  0.0 126.7 jit_solution(8515093277486550331)
XLA Ops:
  0.0 124.8 %shard_map.37 = f32[2,256,256]{2,1,0:T(8,128)} custom-call(f32[2,256,256]{2,1,0:T(8,128)} %bitcast.7, f32[2,256,256]{2,1,0:T(8,128)} %bitcast.8, f32[256,256]{1,0:T(8,128)} %bitcast.9), custom_call_target="tpu_custom_call" | custom-call | tf_op jit(solution)/shard_map/pallas_call | solution.py:360
  124.8 1.9 %copy.6 = f32[1,2,1,256,256]{4,3,2,1,0:T(8,128)} copy(f32[1,2,1,256,256]{4,3,2,1,0:T(8,128)} %bitcast.6) | data formatting | bytes 1048576

commit v3 on v2

--- a/solution.py
+++ b/solution.py
@@ -60,9 +60,9 @@
 
 
 def sweep(nt, nc, nx, state, coupling, inverse, out,
-          flip, wide, inv_far, h_far, a_far, x_near, own, acc,
+          flip, wide, inv_far, h_far, a_far, a_near, x_near, own, acc,
           left_hi, left_lo, right_hi, right_lo, tmp_hi, tmp_lo,
-          send_sems, flip_sems, wide_sems, far_sems, near_sems):
+          send_sems, flip_sems, wide_sems, far_sems, near_sems, go):
     order = inverse.shape[-1]
     piece = order // nx
     per_plane = 2 * nx
@@ -100,6 +100,10 @@
         for step in range(1, s + 1):
             greet(role[s], other, (other + step) % nc)
             expect((col == (row + step) % nc) & (other >= 0) & (row + step <= last))
+            near = (col == (row + step) % nc) & (other >= 0) & (row + step <= last)
+            apart = (row + step) % nc != other % nc
+            greet(role[s] & apart, row, (row + step) % nc)
+            expect(near & apart)
             greet(role[s], row + step, col)
             greet(role[s], row, (col + step) % nc)
         for step in range(1, FRONTS - s):
@@ -111,6 +115,9 @@
     greet((col == 0) & (row < last), row, nc - 1)
     expect((col == nc - 1) & (row < last))
     every = row >= 0
+    first_col = (last - row) % nc
+    greet(col != first_col, row, first_col)
+    greeted.append(jnp.where(role[0], nc - 1, 0))
     for step in (1, nc - 1):
         greet(every, row, (col + step) % nc)
         expect(every)
@@ -133,12 +140,29 @@
             posted.send((col == (row + step) % nc) & (other >= 0) & (row + step <= last),
                         coupling.at[(row + step) // nc % 2], a_far.at[step - 1], far_sems.at[1 + step],
                         other, row % nc)
-
-    for u in range(2):
-        used = nc * u + col > row
-        posted.send(used & (col != nc - 1) & (2 * col != nc - 2), coupling.at[u], flip.at[1, 1 - u],
-                    flip_sems.at[1, 1 - u], row, nc - 2 - col)
-    posted.send((col == nc - 1) & (last > row), coupling.at[1], flip.at[0, 0], flip_sems.at[0, 0], row, 0)
+            apart = (row + step) % nc != other % nc
+            holder = (col == (row + step) % nc) & (other >= 0) & (row + step <= last)
+            posted.send(holder & apart, coupling.at[(row + step) // nc % 2], a_near.at[step - 1],
+                        far_sems.at[3 + step], row, other % nc)
+
+            @pl.when(holder & ~apart)
+            def _():
+                a_near[step - 1] = coupling[(row + step) // nc % 2]
+
+    solver = role[0] | role[1] | role[2]
+
+    flip_local = (2 * col == nc - 2) | (col == nc - 1)
+
+    def reflect(now):
+        for u in range(2):
+            used = nc * u + col > row
+            posted.send(now & used & ~flip_local, coupling.at[u], flip.at[1, 1 - u],
+                        flip_sems.at[1, 1 - u], row, nc - 2 - col)
+            beside = (2 * col == nc - 4) if u == 1 else (2 * col == nc - 4) | (col == nc - 2)
+            to = jnp.where(col == nc - 2, 0, 1) if u == 0 else 0
+            posted.send(now & used & beside, coupling.at[u], flip.at[2, to], flip_sems.at[2, to], row, (col + 1) % nc)
+        posted.send(now & (col == nc - 1) & (last > row), coupling.at[1], flip.at[0, 0], flip_sems.at[0, 0], row, 0)
+
     for u in range(2):
         @pl.when((nc * u + col > row) & (2 * col == nc - 2))
         def _():
@@ -148,11 +172,7 @@
     def _():
         flip[1, 0] = coupling[0]
 
-    solver = role[0] | role[1] | role[2]
-    flip_local = (2 * col == nc - 2) | (col == nc - 1)
-
-    def hand_on(early):
-        now = ~role[0] if early else role[0]
+    def hand_on(now):
         for t in range(2):
             held = source_row(1, t) > row
 
@@ -162,11 +182,8 @@
             up = t + jnp.where(col == nc - 1, 1, 0)
             posted.send(now & held, flip.at[1, t], flip.at[0, up % 2], flip_sems.at[0, up % 2],
                         row, (col + 1) % nc)
-            down = t - jnp.where(col == 0, 1, 0)
-            posted.send(now & held & (down >= 0), flip.at[1, t], flip.at[2, down % 2],
-                        flip_sems.at[2, down % 2], row, (col + nc - 1) % nc)
-
-    hand_on(True)
+            posted.send(now & held & (col != 0) & (2 * col != nc), flip.at[1, t], flip.at[2, t],
+                        flip_sems.at[2, t], row, (col + nc - 1) % nc)
 
     eye = (lax.broadcasted_iota(jnp.int32, (order, order), 0)
            == lax.broadcasted_iota(jnp.int32, (order, order), 1)).astype(F32)
@@ -204,6 +221,17 @@
         def _():
             landed(h_far, far_sems.at[0])
         acc[...] = state[slot] + h_far[...].T
+
+    for step in range(1, nc):
+        @pl.when(role[0])
+        def _():
+            pl.semaphore_signal(go, inc=1, device_id=(row, (col + step) % nc), device_id_type=MESH)
+
+    @pl.when(~role[0])
+    def _():
+        pl.semaphore_wait(go, 1)
+    reflect(~role[0])
+    hand_on(~solver)
 
     def transposed(ref):
         return split(ref[...].T)
@@ -290,17 +318,14 @@
     def _():
         solve()
     spread(0)
-    hand_on(False)
+    reflect(role[0])
+    hand_on(role[0])
     relay(0)
 
-    for t in range(2):
-        for s in (0, 2):
-            flip_wait(s, t)
-
-    exists_row = row + 1 <= last
     @pl.when(role[1])
     def _():
-        left = split(flip[0, slot])
+        landed(a_near.at[0], far_sems.at[4])
+        left = split(a_near[0])
         landed(a_far.at[0], far_sems.at[2])
         tmp_hi[...], tmp_lo[...] = transposed(a_far.at[0])
         landed(x_near.at[0], near_sems.at[0])
@@ -309,6 +334,7 @@
         acc[...] -= product(split(x_near[1]), (tmp_hi[...], tmp_lo[...]))
         solve()
     spread(1)
+    hand_on(role[1])
     relay(1)
 
     @pl.when(role[2])
@@ -316,23 +342,31 @@
         landed(a_far.at[1], far_sems.at[3])
         tmp_hi[...], tmp_lo[...] = transposed(a_far.at[1])
         landed(x_near.at[2], near_sems.at[2])
-        acc[...] -= product(split(flip[0, slot]), split(x_near[2]))
+        landed(a_near.at[1], far_sems.at[5])
+        acc[...] -= product(split(a_near[1]), split(x_near[2]))
         landed(x_near.at[3], near_sems.at[3])
         acc[...] -= product(split(x_near[3]), (tmp_hi[...], tmp_lo[...]))
         landed(a_far.at[0], far_sems.at[2])
         tmp_hi[...], tmp_lo[...] = transposed(a_far.at[0])
-        left = split(flip[1, slot])
+
+        @pl.when((row + 1) % nc != col)
+        def _():
+            landed(a_near.at[0], far_sems.at[4])
+        left = split(a_near[0])
         landed(x_near.at[0], near_sems.at[0])
         acc[...] -= product(left, split(x_near[0]))
         landed(x_near.at[1], near_sems.at[1])
         acc[...] -= product(split(x_near[1]), (tmp_hi[...], tmp_lo[...]))
         solve()
     spread(2)
+    hand_on(role[2])
 
     for s in range(FRONTS):
         if s == FRONTS - 1:
             relay(s)
         for t in range(2):
+            if s != 1:
+                flip_wait(s, t)
             leaf_wait(s, t)
 
             @pl.when(lags[t] >= FRONTS)
@@ -368,6 +402,7 @@
             pltpu.VMEM(tile, F32),
             pltpu.VMEM(tile, F32),
             pltpu.VMEM((2,) + tile, F32),
+            pltpu.VMEM((2,) + tile, F32),
             pltpu.VMEM((4,) + tile, F32),
             pltpu.VMEM(tile, F32),
             pltpu.VMEM(tile, F32),
@@ -380,8 +415,9 @@
             dma((N_SENDS,)),
             dma((FRONTS, 2)),
             dma((FRONTS, 2, nx)),
+            dma((6,)),
             dma((4,)),
-            dma((4,)),
+            pltpu.SemaphoreType.REGULAR,
         ],
         compiler_params=pltpu.CompilerParams(collective_id=0, has_side_effects=True),
     )(state.reshape((2,) + tile), a_tiles.reshape((2,) + tile), inverses.reshape(tile))

time: 127 us -> 123 us (0.969)
  Pallas kernels: 125 us -> 121 us
    pallas_call x1, Pallas kernels: 125 us -> 121 us  [per_device(): pl.pallas_call(functools.partial(sweep, nt, nc, nx), out_shape=jax.ShapeD...]
where the time goes in v3:
time: 123 us
  Pallas kernels  121 us (98%)
  local copies, waits for them, and re-layouts  1.87 us (2%)
    pallas_call x1, Pallas kernels, per_device(): pl.pallas_call(functools.partial(sweep, nt, nc, nx), out_shape=jax.ShapeD...  121 us

profile of v3, /device:TPU:1, one launch (start us, length us, event | category | flops | bytes accessed | tf_op | source)
XLA Modules:
  0.0 123.3 jit_solution(16480665234628174877)
XLA Ops:
  0.0 121.4 %shard_map.37 = f32[2,256,256]{2,1,0:T(8,128)} custom-call(f32[2,256,256]{2,1,0:T(8,128)} %bitcast.7, f32[2,256,256]{2,1,0:T(8,128)} %bitcast.8, f32[256,256]{1,0:T(8,128)} %bitcast.9), custom_call_target="tpu_custom_call" | custom-call | tf_op jit(solution)/shard_map/pallas_call | solution.py:394
  121.4 1.9 %copy.6 = f32[1,2,1,256,256]{4,3,2,1,0:T(8,128)} copy(f32[1,2,1,256,256]{4,3,2,1,0:T(8,128)} %bitcast.6) | data formatting | bytes 1048576

commit v4 on v3

--- a/solution.py
+++ b/solution.py
@@ -100,10 +100,9 @@
         for step in range(1, s + 1):
             greet(role[s], other, (other + step) % nc)
             expect((col == (row + step) % nc) & (other >= 0) & (row + step <= last))
-            near = (col == (row + step) % nc) & (other >= 0) & (row + step <= last)
-            apart = (row + step) % nc != other % nc
-            greet(role[s] & apart, row, (row + step) % nc)
-            expect(near & apart)
+            if s == 1:
+                greet(role[s], row, (row + step) % nc)
+                expect((col == (row + step) % nc) & (other >= 0) & (row + step <= last))
             greet(role[s], row + step, col)
             greet(role[s], row, (col + step) % nc)
         for step in range(1, FRONTS - s):
@@ -131,24 +130,20 @@
     expect(every)
     pl.semaphore_wait(barrier, functools.reduce(lambda x, y: x + y, greeted))
 
-    for s in range(FRONTS):
+    def fetch(s, now):
         other = last - s - row
-        posted.send(role[s] & (other != row), state.at[slot], h_far, far_sems.at[0], other, row % nc)
-        posted.send((col == row % nc) & (other >= 0) & (other != row),
+        posted.send(now & role[s] & (other != row), state.at[slot], h_far, far_sems.at[0], other, row % nc)
+        posted.send(now & (col == row % nc) & (other >= 0) & (other != row),
                     inverse, inv_far, far_sems.at[1], other, col)
         for step in range(1, s + 1):
-            posted.send((col == (row + step) % nc) & (other >= 0) & (row + step <= last),
-                        coupling.at[(row + step) // nc % 2], a_far.at[step - 1], far_sems.at[1 + step],
-                        other, row % nc)
-            apart = (row + step) % nc != other % nc
-            holder = (col == (row + step) % nc) & (other >= 0) & (row + step <= last)
-            posted.send(holder & apart, coupling.at[(row + step) // nc % 2], a_near.at[step - 1],
-                        far_sems.at[3 + step], row, other % nc)
-
-            @pl.when(holder & ~apart)
-            def _():
-                a_near[step - 1] = coupling[(row + step) // nc % 2]
-
+            holder = now & (col == (row + step) % nc) & (other >= 0) & (row + step <= last)
+            tile = coupling.at[(row + step) // nc % 2]
+            if s == 1:
+                posted.send(holder, tile, a_near, far_sems.at[4], row, other % nc)
+            posted.send(holder, tile, a_far.at[step - 1], far_sems.at[1 + step], other, row % nc)
+
+    fetch(0, every)
+    fetch(1, every)
     solver = role[0] | role[1] | role[2]
 
     flip_local = (2 * col == nc - 2) | (col == nc - 1)
@@ -202,8 +197,7 @@
     self_mirror = role[1] & (2 * row == last - 1)
     mirrored = solver & ~self_mirror
 
-    @pl.when(solver)
-    def _():
+    def prepare():
         powers(eye - 0.5 * inverse[...], left_hi, left_lo)
 
         @pl.when(mirrored)
@@ -222,6 +216,10 @@
             landed(h_far, far_sems.at[0])
         acc[...] = state[slot] + h_far[...].T
 
+    @pl.when(role[0])
+    def _():
+        prepare()
+
     for step in range(1, nc):
         @pl.when(role[0])
         def _():
@@ -230,8 +228,13 @@
     @pl.when(~role[0])
     def _():
         pl.semaphore_wait(go, 1)
+    fetch(2, ~role[0])
     reflect(~role[0])
     hand_on(~solver)
+
+    @pl.when(role[1] | role[2])
+    def _():
+        prepare()
 
     def transposed(ref):
         return split(ref[...].T)
@@ -307,25 +310,26 @@
             for q in range(nx):
                 landed(wide.at[s, t, pl.ds(q * piece, piece)], wide_sems.at[s, t, q])
 
-    def flip_wait(s, t):
+    def flip_wait(s, t, now):
         held = source_row(s, t) > row
-        if s != 1:
-            @pl.when(held)
-            def _():
-                landed(flip.at[s, t], flip_sems.at[s, t])
+
+        @pl.when(now & held)
+        def _():
+            landed(flip.at[s, t], flip_sems.at[s, t])
 
     @pl.when(role[0])
     def _():
         solve()
     spread(0)
+    fetch(2, role[0])
     reflect(role[0])
     hand_on(role[0])
     relay(0)
 
     @pl.when(role[1])
     def _():
-        landed(a_near.at[0], far_sems.at[4])
-        left = split(a_near[0])
+        landed(a_near, far_sems.at[4])
+        left = split(a_near[...])
         landed(a_far.at[0], far_sems.at[2])
         tmp_hi[...], tmp_lo[...] = transposed(a_far.at[0])
         landed(x_near.at[0], near_sems.at[0])
@@ -336,37 +340,34 @@
     spread(1)
     hand_on(role[1])
     relay(1)
+    hand_on(role[2])
+    for t in range(2):
+        flip_wait(0, t, role[2])
 
     @pl.when(role[2])
     def _():
         landed(a_far.at[1], far_sems.at[3])
         tmp_hi[...], tmp_lo[...] = transposed(a_far.at[1])
         landed(x_near.at[2], near_sems.at[2])
-        landed(a_near.at[1], far_sems.at[5])
-        acc[...] -= product(split(a_near[1]), split(x_near[2]))
+        acc[...] -= product(split(flip[0, slot]), split(x_near[2]))
         landed(x_near.at[3], near_sems.at[3])
         acc[...] -= product(split(x_near[3]), (tmp_hi[...], tmp_lo[...]))
         landed(a_far.at[0], far_sems.at[2])
         tmp_hi[...], tmp_lo[...] = transposed(a_far.at[0])
-
-        @pl.when((row + 1) % nc != col)
-        def _():
-            landed(a_near.at[0], far_sems.at[4])
-        left = split(a_near[0])
+        left = split(flip[1, slot])
         landed(x_near.at[0], near_sems.at[0])
         acc[...] -= product(left, split(x_near[0]))
         landed(x_near.at[1], near_sems.at[1])
         acc[...] -= product(split(x_near[1]), (tmp_hi[...], tmp_lo[...]))
         solve()
     spread(2)
-    hand_on(role[2])
 
     for s in range(FRONTS):
         if s == FRONTS - 1:
             relay(s)
         for t in range(2):
             if s != 1:
-                flip_wait(s, t)
+                flip_wait(s, t, ~role[2] if s == 0 else every)
             leaf_wait(s, t)
 
             @pl.when(lags[t] >= FRONTS)
@@ -402,7 +403,7 @@
             pltpu.VMEM(tile, F32),
             pltpu.VMEM(tile, F32),
             pltpu.VMEM((2,) + tile, F32),
-            pltpu.VMEM((2,) + tile, F32),
+            pltpu.VMEM(tile, F32),
             pltpu.VMEM((4,) + tile, F32),
             pltpu.VMEM(tile, F32),
             pltpu.VMEM(tile, F32),
@@ -415,7 +416,7 @@
             dma((N_SENDS,)),
             dma((FRONTS, 2)),
             dma((FRONTS, 2, nx)),
-            dma((6,)),
+            dma((5,)),
             dma((4,)),
             pltpu.SemaphoreType.REGULAR,
         ],

time: 123 us -> 117 us (0.951)
  Pallas kernels: 121 us -> 115 us
    pallas_call x1, Pallas kernels: 121 us -> 115 us  [per_device(): pl.pallas_call(functools.partial(sweep, nt, nc, nx), out_shape=jax.ShapeD...]
where the time goes in v4:
time: 117 us
  Pallas kernels  115 us (98%)
  local copies, waits for them, and re-layouts  1.87 us (2%)
    pallas_call x1, Pallas kernels, per_device(): pl.pallas_call(functools.partial(sweep, nt, nc, nx), out_shape=jax.ShapeD...  115 us

profile of v4, /device:TPU:1, one launch (start us, length us, event | category | flops | bytes accessed | tf_op | source)
XLA Modules:
  0.0 116.9 jit_solution(13905283897569025264)
XLA Ops:
  0.0 115.0 %shard_map.37 = f32[2,256,256]{2,1,0:T(8,128)} custom-call(f32[2,256,256]{2,1,0:T(8,128)} %bitcast.7, f32[2,256,256]{2,1,0:T(8,128)} %bitcast.8, f32[256,256]{1,0:T(8,128)} %bitcast.9), custom_call_target="tpu_custom_call" | custom-call | tf_op jit(solution)/shard_map/pallas_call | solution.py:395
  115.0 1.9 %copy.6 = f32[1,2,1,256,256]{4,3,2,1,0:T(8,128)} copy(f32[1,2,1,256,256]{4,3,2,1,0:T(8,128)} %bitcast.6) | data formatting | bytes 1048576
